TPU v7x, 512 devices: a whole 4x8x8 slice. The times are simulated.
512 devices in a mesh: dp: 16 (over z, core), expert: 32 (over x, y).
Axes of the slice: x: 4, y: 8, z: 8, core: 2. Of those that a mesh axis runs over, the one named last changes fastest.
Arguments:
- pivot_states: bfloat16 [65536, 2048], P(('dp', 'expert')), may hold values from -6 to 6
- queries: bfloat16 [65536, 2048], P(('dp', 'expert')), may hold values from -8 to 8
- keys: bfloat16 [65536, 2048], P(('dp', 'expert')), may hold values from -8 to 8
- values: bfloat16 [65536, 2048], P(('dp', 'expert')), may hold values from -6 to 6
- pack_pos: int32 [65536], P(('dp', 'expert')), may hold values from 0 to 2047, as said below
- segment_ids: int32 [512, 128], P(('dp', 'expert')), may hold values from 0 to 7, never falling along the last dimension, each value on 1 to 64 neighbouring positions
- expert_ids: int32 [65536, 2], P(('dp', 'expert')), may hold values from 0 to 127, all different within a row
- gate_code: int32 [65536, 2], P(('dp', 'expert')), may hold values from 6554 to 65535
- ln_gain: float32 [2048], replicated, may hold values from 0.5 to 1.5
- ln_bias: float32 [2048], replicated, may hold values from -3 to 3
- w_in: bfloat16 [32, 2048, 4096], P('expert', None, 'dp'), may hold values from -0.125 to 0.125
- b_in: float32 [32, 4096], P('expert', 'dp'), may hold values from -3 to 3
- w_out: bfloat16 [32, 4096, 2048], P('expert', 'dp'), may hold values from -0.09375 to 0.09375
- b_out: float32 [32, 2048], replicated, may hold values from -3 to 3
Outputs:
- layer_out: bfloat16 [65536, 2048], P(('dp', 'expert'))
Inputs may be any that keep to these rules, and one draw needn't show every extreme that they name: Within one index of expert, pack_pos over the devices of dp is a permutation, and each device's tokens go exactly 8 to each packed block of its column. `expert_ids`: only ids below 32 belong to the experts of this round.
All inputs are finite; a program needn't handle non-finite values.
Results may differ from a plain program's by a relative error of at most 0.0055.
Values may be sent and summed in bfloat16 or wider, within the bound.
A program may use at most 64 MiB of HBM per device.

v0:
```python
import math
import jax
import jax.numpy as jnp
from jax import lax
from jax.sharding import PartitionSpec as P

HEAD_DIM = 128
ROUNDS = 4
epsilon = 1e-05
mask_fill = -1e30


def per_device(
    pivot_states,
    queries,
    keys,
    values,
    pack_pos,
    segment_ids,
    expert_ids,
    gate_code,
    ln_gain,
    ln_bias,
    w_in,
    b_in,
    w_out,
    b_out,
):
    tok_count = pivot_states.shape[0]
    model_width = pivot_states.shape[1]
    dp_count = lax.axis_size("dp")
    expert_count = lax.axis_size("expert")
    per_target = tok_count // dp_count
    target_block = pack_pos // tok_count
    offsets = pack_pos % tok_count
    target_hot = (target_block[:, None] == jnp.arange(dp_count, dtype=jnp.int32)[None, :]).astype(
        jnp.int32
    )
    bucket_rank = jnp.sum(jnp.cumsum(target_hot, axis=0) * target_hot, axis=1) - 1
    send_index = target_block * per_target + bucket_rank
    joined = jnp.concatenate([pivot_states, queries, keys, values], axis=1)
    send_rows = jnp.zeros_like(joined).at[send_index].set(joined)
    send_offsets = jnp.zeros_like(offsets).at[send_index].set(offsets)
    recv_rows, recv_offsets = (
        lax.all_to_all(send_rows, "dp", split_axis=0, concat_axis=0, tiled=True),
        lax.all_to_all(send_offsets, "dp", split_axis=0, concat_axis=0, tiled=True),
    )
    packed = jnp.zeros_like(recv_rows).at[recv_offsets].set(recv_rows)
    state_rows = packed[:, :model_width]
    query_rows = packed[:, model_width : 2 * model_width]
    key_rows = packed[:, 2 * model_width : 3 * model_width]
    value_rows = packed[:, 3 * model_width :]
    head_count = model_width // HEAD_DIM
    key_heads = key_rows.reshape(tok_count, head_count, HEAD_DIM)
    value_heads = value_rows.reshape(tok_count, head_count, HEAD_DIM)
    seg_row = segment_ids[0]
    block_rows = min(tok_count, 512)
    block_count = tok_count // block_rows
    score_scale = 1.0 / math.sqrt(HEAD_DIM)

    def attend(block_args):
        query_block, seg_block = block_args
        query_heads = query_block.reshape(block_rows, head_count, HEAD_DIM)
        scores = (
            jnp.einsum("qhd,khd->hqk", query_heads, key_heads, preferred_element_type=jnp.float32)
            * score_scale
        )
        same_doc = seg_block[:, None] == seg_row[None, :]
        scores = jnp.where(same_doc[None, :, :], scores, mask_fill)
        top_score = jnp.max(scores, axis=2, keepdims=True)
        exp_terms = jnp.exp(scores - top_score)
        softmax_weights = (exp_terms / jnp.sum(exp_terms, axis=2, keepdims=True)).astype(
            jnp.bfloat16
        )
        mixed_heads = jnp.einsum(
            "hqk,khd->qhd", softmax_weights, value_heads, preferred_element_type=jnp.float32
        )
        return mixed_heads.reshape(block_rows, model_width)

    attended = lax.map(
        attend,
        (
            query_rows.reshape(block_count, block_rows, model_width),
            seg_row.reshape(block_count, block_rows),
        ),
    )
    hidden_state = state_rows.astype(jnp.float32) + attended.reshape(tok_count, model_width)
    mean_value = jnp.mean(hidden_state, axis=1, keepdims=True)
    centered = hidden_state - mean_value
    variance = jnp.mean(centered * centered, axis=1, keepdims=True)
    normed = (centered * lax.rsqrt(variance + epsilon) * ln_gain + ln_bias).astype(jnp.bfloat16)
    capacity = max(2, 2 * tok_count // (ROUNDS * expert_count))
    assigned = jnp.concatenate([expert_ids[:, 0], expert_ids[:, 1]])
    expert_hot = (assigned[:, None] == jnp.arange(expert_count, dtype=jnp.int32)[None, :]).astype(
        jnp.int32
    )
    slot_rank = jnp.sum(jnp.cumsum(expert_hot, axis=0) * expert_hot, axis=1) - 1
    kept_mask = (assigned < expert_count) & (slot_rank < capacity)
    overflow = expert_count * capacity
    slot_index = jnp.where(kept_mask, assigned * capacity + slot_rank, overflow)
    buffer = jnp.zeros((overflow, model_width), jnp.bfloat16)
    buffer = (
        buffer.at[slot_index[:tok_count]]
        .set(normed, mode="drop")
        .at[slot_index[tok_count:]]
        .set(normed, mode="drop")
    )
    first_matrix = w_in[0]
    bias_in_row = b_in[0]
    second_matrix = w_out[0]
    arrived = lax.all_to_all(
        buffer.reshape(expert_count, capacity, model_width),
        "expert",
        split_axis=0,
        concat_axis=0,
        tiled=True,
    )
    arrived = arrived.reshape(overflow, model_width)
    hidden = jnp.dot(
        lax.all_gather(arrived, "dp", axis=0, tiled=True),
        first_matrix,
        preferred_element_type=jnp.float32,
    )
    hidden = jnp.maximum(hidden + bias_in_row, 0.0).astype(jnp.bfloat16)
    partial_value = jnp.dot(hidden, second_matrix, preferred_element_type=jnp.float32).astype(
        jnp.bfloat16
    )
    summed = lax.psum(partial_value, "dp").astype(jnp.float32)
    summed = lax.dynamic_slice_in_dim(summed, lax.axis_index("dp") * overflow, overflow, 0)
    bias_out_row = lax.dynamic_slice_in_dim(b_out, lax.axis_index("expert"), 1, 0)
    results = (summed + bias_out_row).astype(jnp.bfloat16)
    returned = lax.all_to_all(
        results.reshape(expert_count, capacity, model_width),
        "expert",
        split_axis=0,
        concat_axis=0,
        tiled=True,
    )
    returned = returned.reshape(overflow, model_width)
    gate_values = gate_code.astype(jnp.float32) / 65536.0
    gate_flat = jnp.concatenate([gate_values[:, 0], gate_values[:, 1]])
    weights = jnp.where(kept_mask, gate_flat, 0.0)
    guard_index = jnp.minimum(slot_index, overflow - 1)
    picked = returned[guard_index].astype(jnp.float32) * weights[:, None]
    layer_out = hidden_state + picked[:tok_count] + picked[tok_count:]
    return layer_out.astype(jnp.bfloat16)


def solution(mesh):
    return jax.shard_map(
        per_device,
        mesh=mesh,
        in_specs=(
            P(("dp", "expert"), None),
            P(("dp", "expert"), None),
            P(("dp", "expert"), None),
            P(("dp", "expert"), None),
            P(("dp", "expert")),
            P(("dp", "expert"), None),
            P(("dp", "expert"), None),
            P(("dp", "expert"), None),
            P(),
            P(),
            P("expert", None, "dp"),
            P("expert", "dp"),
            P("expert", "dp", None),
            P(),
        ),
        out_specs=P(("dp", "expert"), None),
        check_vma=False,
    )
```

profile of v0, /device:TPU:8, one launch (start us, length us, event | category | flops | bytes accessed | tf_op | source)
XLA Modules:
  0.0 335.2 jit_solution(7050097430861302124)
XLA Ops:
  6.5 0.0 copy-start
  6.5 0.8 and_select_fusion.1
  7.3 0.1 fusion.28
  7.4 0.2 reduce_window_sum.26
  7.6 0.2 select_reduce_fusion
  7.7 1.0 scatter_custom_fusion
  8.7 0.7 all_to_all.22
  9.4 10.4 %all-to-all-start = ((s32[16,8,1]{1,2,0:T(1,128)}), s32[16,8,1]{1,2,0:T(1,128)S(1)}, u32[]{:S(2)}, u32[]{:S(2)}) async-start(s32[16,8,1]{1,2,0:T(1,128)} %bitcast), calls=%async_computation | async-start | bytes 16384 | tf_op jit(solution)/shard_map/all_to_all | solution.py:46
  19.8 6.0 %scatter_custom_fusion.1 = bf16[128,8192]{1,0:T(8,128)(2,1)} fusion(s32[128]{0:T(128)S(1)} %compare_select_fusion.4, bf16[128,2048]{1,0:T(8,128)(2,1)} %param.17, bf16[]{:T(256)} %constant.122, bf16[128,2048]{1,0:T(8,128)(2,1)} %param.16, bf16[128,2048]{1,0:T(8,128)(2,1)} %param.15, bf16[128,2048]{1,0:T(8,128)(2,1)} %param.14, bf16[]{:T(256)} %constant.46.clone.1), kind=kCustom, calls=%fused_computation.8 | custom fusion | flops 8388608 | bytes 4194308 | tf_op jit(solution)/shard_map/scatter | solution.py:42
  25.8 1.6 all-to-all-done
  27.4 5.8 %all-to-all-start.1 = ((bf16[16,8,8192]{2,1,0:T(8,128)(2,1)}), bf16[16,8,8192]{2,1,0:T(8,128)(2,1)}, u32[]{:S(2)}, u32[]{:S(2)}) async-start(bf16[16,8,8192]{2,1,0:T(8,128)(2,1)} %bitcast.2), calls=%async_computation.1 | async-start | bytes 4194304 | tf_op jit(solution)/shard_map/all_to_all | solution.py:45
  33.2 0.0 all-gather.2.cloned.1.call-start
  33.3 0.0 copy-done.6
  33.3 0.6 reduce-window.6
  33.9 0.2 slice_reduce_fusion
  34.1 0.1 fusion.30
  34.3 0.0 copy-done.5
  34.3 0.1 broadcast_compare_fusion
  34.4 0.5 broadcast.249
  34.9 0.7 reduce.5
  35.6 0.1 all_to_all.24
  35.7 46.8 %all-to-all-done.1 = bf16[16,8,8192]{2,1,0:T(8,128)(2,1)} async-done(((bf16[16,8,8192]{2,1,0:T(8,128)(2,1)}), bf16[16,8,8192]{2,1,0:T(8,128)(2,1)}, u32[]{:S(2)}, u32[]{:S(2)}) %all-to-all-start.1) | async-done | bytes 2097184 | tf_op jit(solution)/shard_map/all_to_all | solution.py:45
  82.5 5.2 %scatter_custom_fusion.2 = bf16[128,8192]{1,0:T(8,128)(2,1)S(1)} fusion(s32[128]{0:T(128)S(1)} %fusion.32, bf16[16,8,8192]{2,1,0:T(8,128)(2,1)} %all-to-all-done.1, bf16[]{:T(256)} %constant.46.clone.1), kind=kCustom, calls=%fused_computation.16 | custom fusion | bytes 4194306 | tf_op jit(solution)/shard_map/scatter | solution.py:48
  87.7 0.0 copy-start.1
  87.7 1.3 fusion.39
  89.0 2.1 copy.28
  91.0 0.0 copy-done.1
  91.0 1.4 copy.29
  92.4 1.4 fusion.13
  93.8 0.2 fusion.41
  94.0 0.0 copy-done.2
  94.1 0.3 copy.27
  94.3 1.4 fusion.22
  95.8 1.6 copy.33
  97.3 0.0 copy-start.3
  97.3 0.0 copy-start.4
  97.3 1.2 fusion.38
  98.6 1.3 multiply_reduce_fusion
  99.9 0.0 copy-done.3
  99.9 0.0 copy-done.4
  99.9 1.3 add_convert_fusion
  101.2 1.4 scatter_custom_fusion.3
  102.6 0.0 copy-start.8
  102.6 1.5 scatter_fusion
  104.1 0.2 reshape.242
  104.3 22.6 %all_to_all.34 = bf16[32,2,2048]{2,1,0:T(2,128)(2,1)S(1)} all-to-all(bf16[32,2,2048]{2,1,0:T(2,128)(2,1)S(1)} %reshape.242), channel_id=1, replica_groups=mesh['dp'=16,'expert'=32] {'expert'}, dimensions={0} | all-to-all | bytes 524288 | tf_op jit(solution)/shard_map/all_to_all | solution.py:111
  126.9 0.8 reshape.243
  127.7 0.0 all-gather.2.cloned.1.call-update
  127.8 0.0 all-reduce.2.cloned.1.call-start
  127.8 38.2 %all-gather.2.cloned.1.call-done = bf16[1024,2048]{1,0:T(8,128)(2,1)} async-done(((bf16[64,2048]{1,0:T(8,128)(2,1)}), bf16[1024,2048]{1,0:T(8,128)(2,1)}) %all-gather.2.cloned.1.call-update) | async-done | bytes 4194320 | tf_op jit(solution)/shard_map/all_gather | solution.py:120
  166.0 0.0 copy-done.8
  166.0 8.8 %convolution_convert_fusion = bf16[1024,2048]{1,0:T(8,128)(2,1)} fusion(bf16[1024,2048]{1,0:T(8,128)(2,1)} %all-gather.2.cloned.1.call-done, bf16[1,256,2048]{2,1,0:T(8,128)(2,1)S(1)} %copy-done, bf16[1,2048,256]{2,1,0:T(8,128)(2,1)} %param.24, f32[256]{0:T(256)S(1)} %bitcast.65), kind=kOutput, calls=%fused_computation.7 | convolution fusion | flops 2150367232 | bytes 10486784 | tf_op jit(solution)/shard_map/dot_general | solution.py:125
  174.8 0.0 all-reduce.2.cloned.1.call-update
  174.8 0.6 copy-done.7
  175.5 0.9 constant_dynamic-slice_fusion
  176.3 124.8 %all-reduce.2.cloned.1.call-done = bf16[1024,2048]{1,0:T(8,128)(2,1)} async-done(((bf16[1024,2048]{1,0:T(8,128)(2,1)}), bf16[1024,2048]{1,0:T(8,128)(2,1)}) %all-reduce.2.cloned.1.call-update) | async-done | bytes 4194320 | tf_op jit(solution)/shard_map/psum | solution.py:128
  301.2 1.0 add_convert_fusion.1
  302.2 0.9 reshape.244
  303.0 9.8 %all-to-all-start.3 = ((bf16[32,2,2048]{2,1,0:T(2,128)(2,1)}), bf16[32,2,2048]{2,1,0:T(2,128)(2,1)S(1)}, u32[]{:S(2)}, u32[]{:S(2)}) async-start(bf16[32,2,2048]{2,1,0:T(2,128)(2,1)} %reshape.244), calls=%async_computation.3 | async-start | bytes 524288 | tf_op jit(solution)/shard_map/all_to_all | solution.py:132
  312.9 11.5 %all-to-all-done.3 = bf16[32,2,2048]{2,1,0:T(2,128)(2,1)S(1)} async-done(((bf16[32,2,2048]{2,1,0:T(2,128)(2,1)}), bf16[32,2,2048]{2,1,0:T(2,128)(2,1)S(1)}, u32[]{:S(2)}, u32[]{:S(2)}) %all-to-all-start.3) | async-done | bytes 262176 | tf_op jit(solution)/shard_map/all_to_all | solution.py:132
  324.5 0.1 reshape.245
  324.6 1.4 gather_fusion
  325.9 0.2 convert_multiply_fusion
  326.1 2.2 fusion.16
  (21 shorter events, 0.1 us)
Async XLA Ops:
  6.5 159.5 %copy-start = (bf16[1,256,2048]{2,1,0:T(8,128)(2,1)S(1)}, bf16[1,256,2048]{2,1,0:T(8,128)(2,1)}, u32[]{:S(2)}) copy-start(bf16[1,256,2048]{2,1,0:T(8,128)(2,1)} %param.26) | copy-start | bytes 3145732
  9.4 18.0 %all-to-all-start = ((s32[16,8,1]{1,2,0:T(1,128)}), s32[16,8,1]{1,2,0:T(1,128)S(1)}, u32[]{:S(2)}, u32[]{:S(2)}) async-start(s32[16,8,1]{1,2,0:T(1,128)} %bitcast), calls=%async_computation | async-start | bytes 16384 | tf_op jit(solution)/shard_map/all_to_all | solution.py:46
  27.4 5.9 %copy-start.6 = (s32[128,2]{0,1:T(2,128)S(1)}, s32[128,2]{0,1:T(2,128)}, u32[]{:S(2)}) copy-start(s32[128,2]{0,1:T(2,128)} %param.20) | copy-start | bytes 3076
  27.4 6.9 %copy-start.5 = (s32[1,128]{1,0:T(1,128)S(1)}, s32[1,128]{1,0:T(1,128)}, u32[]{:S(2)}) copy-start(s32[1,128]{1,0:T(1,128)} %param.19) | copy-start | bytes 1540
  27.4 55.1 %all-to-all-start.1 = ((bf16[16,8,8192]{2,1,0:T(8,128)(2,1)}), bf16[16,8,8192]{2,1,0:T(8,128)(2,1)}, u32[]{:S(2)}, u32[]{:S(2)}) async-start(bf16[16,8,8192]{2,1,0:T(8,128)(2,1)} %bitcast.2), calls=%async_computation.1 | async-start | bytes 4194304 | tf_op jit(solution)/shard_map/all_to_all | solution.py:45
  33.2 132.8 %all-gather.2.cloned.1.call-start = ((), (), s32[]{:S(2)}) async-start(), calls=%async_computation.4 | async-start | bytes 4456448 | tf_op jit(solution)/shard_map/all_gather | solution.py:120
  87.7 3.3 copy-start.1
  91.0 3.0 copy-start.2
  97.3 2.6 copy-start.3
  97.3 2.6 copy-start.4
  102.6 63.4 %copy-start.8 = (f32[1,256]{1,0:T(1,128)S(1)}, f32[1,256]{1,0:T(1,128)}, u32[]{:S(2)}) copy-start(f32[1,256]{1,0:T(1,128)} %param.25) | copy-start | bytes 3076
  127.8 173.4 %all-reduce.2.cloned.1.call-start = ((), (), s32[]{:S(2)}) async-start(), calls=%async_computation.5 | async-start | bytes 8388608 | tf_op jit(solution)/shard_map/psum | solution.py:128
  174.8 0.7 copy-start.7
  303.0 21.4 %all-to-all-start.3 = ((bf16[32,2,2048]{2,1,0:T(2,128)(2,1)}), bf16[32,2,2048]{2,1,0:T(2,128)(2,1)S(1)}, u32[]{:S(2)}, u32[]{:S(2)}) async-start(bf16[32,2,2048]{2,1,0:T(2,128)(2,1)} %reshape.244), calls=%async_computation.3 | async-start | bytes 524288 | tf_op jit(solution)/shard_map/all_to_all | solution.py:132
Sparse Core Ops, SparseCore 0:
  127.9 38.0 all-gather.1
  174.9 126.1 all-reduce.1
where the time goes:
time: 336 us; the launch traced here: 335 us
  waiting for transfers between devices  223 us (66%)
  starting transfers between devices  26.2 us (8%)
  blocking collectives  22.6 us (7%)
  local copies, waits for them, and re-layouts  21.9 us (7%)
  other arithmetic  16.2 us (5%)
  between operations  13.7 us (4%)
  matrix products  11.6 us (3%)
    psum x1, waiting for transfers between devices, per_device(): summed = lax.psum(partial_value, 'dp').astype(jnp.float32)  125 us
    all_to_all x1, waiting for transfers between devices, per_device(): lax.all_to_all(send_rows, 'dp', split_axis=0, concat_axis=0, tiled=True)  46.8 us
    all_gather x1, waiting for transfers between devices, per_device(): lax.all_gather(arrived, 'dp', axis=0, tiled=True)  38.2 us
    all_to_all x1, blocking collectives, per_device(): lax.all_to_all(buffer.reshape(expert_count, capacity, model_width), 'expe...  22.6 us
    all_to_all x1, waiting for transfers between devices, per_device(): lax.all_to_all(results.reshape(expert_count, capacity, model_width), 'exp...  11.5 us
    all_to_all x1, starting transfers between devices, per_device(): lax.all_to_all(send_offsets, 'dp', split_axis=0, concat_axis=0, tiled=True)  10.4 us
    all_to_all x1, starting transfers between devices, per_device(): lax.all_to_all(results.reshape(expert_count, capacity, model_width), 'exp...  9.85 us
    dot_general x1, matrix products, per_device(): jnp.dot(hidden, second_matrix, preferred_element_type=jnp.float32)  8.76 us
  transfers between devices with their start and end apart: 5, of which 5 were waited for; matrix products, arithmetic and copies ran while one was open for 3% of the time, Pallas kernels for 0%

commit v1 on v0

--- a/solution.py
+++ b/solution.py
@@ -8,6 +8,33 @@
 ROUNDS = 4
 epsilon = 1e-05
 mask_fill = -1e30
+
+
+def regions_cover(here_x, axis_k):
+    right_arr, r_now, val2 = (
+        jax.lax.axis_size("dp"),
+        jax.lax.axis_index("dp"),
+        here_x.shape[axis_k],
+    )
+    trail = tuple(((b, (b + 1) % right_arr) for b in range(right_arr)))
+    inbox = tuple(((b, (b - 1) % right_arr) for b in range(right_arr)))
+    upper = jnp.zeros(
+        (*here_x.shape[:axis_k], right_arr * val2, *here_x.shape[axis_k + 1 :]), here_x.dtype
+    )
+    upper = lax.dynamic_update_slice_in_dim(upper, here_x, r_now * val2, axis=axis_k)
+    odd = all_rows = here_x
+    aux = right_arr // 2
+    for dd in [*range(1, aux + 1)]:
+        odd = jax.lax.ppermute(odd, "dp", trail)
+        upper = lax.dynamic_update_slice_in_dim(
+            upper, odd, (r_now - dd) % right_arr * val2, axis=axis_k
+        )
+        if dd < right_arr - aux:
+            all_rows = jax.lax.ppermute(all_rows, axis_name="dp", perm=inbox)
+            upper = lax.dynamic_update_slice_in_dim(
+                upper, all_rows, (r_now + dd) % right_arr * val2, axis=axis_k
+            )
+    return upper
 
 
 def per_device(
@@ -116,11 +143,7 @@
         tiled=True,
     )
     arrived = arrived.reshape(overflow, model_width)
-    hidden = jnp.dot(
-        lax.all_gather(arrived, "dp", axis=0, tiled=True),
-        first_matrix,
-        preferred_element_type=jnp.float32,
-    )
+    hidden = jnp.dot(regions_cover(arrived, 0), first_matrix, preferred_element_type=jnp.float32)
     hidden = jnp.maximum(hidden + bias_in_row, 0.0).astype(jnp.bfloat16)
     partial_value = jnp.dot(hidden, second_matrix, preferred_element_type=jnp.float32).astype(
         jnp.bfloat16

time: 336 us -> 347 us (1.033)
  waiting for transfers between devices: 223 us -> 202 us
  starting transfers between devices: 26.2 us -> 46.7 us
  local copies, waits for them, and re-layouts: 21.9 us -> 34.1 us
    all_gather x1 -> x0, waiting for transfers between devices: 38.2 us -> none  [per_device(): lax.all_gather(arrived, 'dp', axis=0, tiled=True)]
    ppermute x0 -> x15, waiting for transfers between devices: none -> 22 us  [the longest x8 22 us: regions_cover(): odd = jax.lax.ppermute(odd, 'dp', trail)]
    ppermute x0 -> x15, starting transfers between devices: none -> 20.7 us  [the longest x7 20.7 us: regions_cover(): all_rows = jax.lax.ppermute(all_rows, axis_name='dp', perm=inbox)]
    dynamic_update_slice x0 -> x16, local copies, waits for them, and re-layouts: none -> 11.6 us  [the longest x8 5.78 us: regions_cover(): lax.dynamic_update_slice_in_dim(upper, odd, (r_now - dd) % right_arr * va...]
    psum x1, waiting for transfers between devices: 125 us -> 120 us  [per_device(): summed = lax.psum(partial_value, 'dp').astype(jnp.float32)]
  transfers between devices with their start and end apart: 5 -> 19, of which waited for: 5 -> 12; matrix products, arithmetic and copies ran while one was open for 3% -> 6% of each run, Pallas kernels for 0% -> 0%
where the time goes in v1:
time: 347 us
  waiting for transfers between devices  202 us (58%)
  starting transfers between devices  46.7 us (13%)
  local copies, waits for them, and re-layouts  34.1 us (10%)
  blocking collectives  22.6 us (7%)
  other arithmetic  16.1 us (5%)
  between operations  13.7 us (4%)
  matrix products  11.6 us (3%)
    psum x1, waiting for transfers between devices, per_device(): summed = lax.psum(partial_value, 'dp').astype(jnp.float32)  120 us
    all_to_all x1, waiting for transfers between devices, per_device(): lax.all_to_all(send_rows, 'dp', split_axis=0, concat_axis=0, tiled=True)  46.8 us
    all_to_all x1, blocking collectives, per_device(): lax.all_to_all(buffer.reshape(expert_count, capacity, model_width), 'expe...  22.6 us
    ppermute x8, waiting for transfers between devices, regions_cover(): odd = jax.lax.ppermute(odd, 'dp', trail)  22 us
    ppermute x7, starting transfers between devices, regions_cover(): all_rows = jax.lax.ppermute(all_rows, axis_name='dp', perm=inbox)  20.7 us
    all_to_all x1, waiting for transfers between devices, per_device(): lax.all_to_all(results.reshape(expert_count, capacity, model_width), 'exp...  11.5 us
    all_to_all x1, starting transfers between devices, per_device(): lax.all_to_all(send_offsets, 'dp', split_axis=0, concat_axis=0, tiled=True)  10.4 us
    all_to_all x1, starting transfers between devices, per_device(): lax.all_to_all(results.reshape(expert_count, capacity, model_width), 'exp...  9.85 us
  transfers between devices with their start and end apart: 19, of which 12 were waited for; matrix products, arithmetic and copies ran while one was open for 6% of the time, Pallas kernels for 0%

profile of v1, /device:TPU:8, one launch (start us, length us, event | category | flops | bytes accessed | tf_op | source)
XLA Modules:
  0.0 346.5 jit_solution(18161031207822831715)
XLA Ops:
  6.5 0.8 and_select_fusion.1
  7.7 1.0 scatter_custom_fusion
  8.7 0.7 all_to_all.22
  9.4 10.4 %all-to-all-start = ((s32[16,8,1]{1,2,0:T(1,128)}), s32[16,8,1]{1,2,0:T(1,128)S(1)}, u32[]{:S(2)}, u32[]{:S(2)}) async-start(s32[16,8,1]{1,2,0:T(1,128)} %bitcast), calls=%async_computation | async-start | bytes 16384 | tf_op jit(solution)/shard_map/all_to_all | solution.py:73
  19.9 6.0 %scatter_custom_fusion.1 = bf16[128,8192]{1,0:T(8,128)(2,1)} fusion(s32[128]{0:T(128)S(1)} %compare_select_fusion.4, bf16[128,2048]{1,0:T(8,128)(2,1)} %param.17, bf16[]{:T(256)} %constant.218, bf16[128,2048]{1,0:T(8,128)(2,1)} %param.16, bf16[128,2048]{1,0:T(8,128)(2,1)} %param.15, bf16[128,2048]{1,0:T(8,128)(2,1)} %param.14, bf16[]{:T(256)} %constant.165.clone.1), kind=kCustom, calls=%fused_computation.8 | custom fusion | flops 8388608 | bytes 4194308 | tf_op jit(solution)/shard_map/scatter | solution.py:69
  25.8 1.5 all-to-all-done
  27.4 5.7 %all-to-all-start.1 = ((bf16[16,8,8192]{2,1,0:T(8,128)(2,1)}), bf16[16,8,8192]{2,1,0:T(8,128)(2,1)}, u32[]{:S(2)}, u32[]{:S(2)}) async-start(bf16[16,8,8192]{2,1,0:T(8,128)(2,1)} %bitcast.57), calls=%async_computation.1 | async-start | bytes 4194304 | tf_op jit(solution)/shard_map/all_to_all | solution.py:72
  33.2 0.6 reduce-window.6
  34.8 0.7 reduce.5
  35.6 46.8 %all-to-all-done.1 = bf16[16,8,8192]{2,1,0:T(8,128)(2,1)} async-done(((bf16[16,8,8192]{2,1,0:T(8,128)(2,1)}), bf16[16,8,8192]{2,1,0:T(8,128)(2,1)}, u32[]{:S(2)}, u32[]{:S(2)}) %all-to-all-start.1) | async-done | bytes 2097184 | tf_op jit(solution)/shard_map/all_to_all | solution.py:72
  82.4 6.0 %scatter_custom_fusion.2 = bf16[128,8192]{1,0:T(8,128)(2,1)} fusion(s32[128]{0:T(128)S(1)} %fusion.32, bf16[16,8,8192]{2,1,0:T(8,128)(2,1)} %all-to-all-done.1, bf16[]{:T(256)} %constant.165.clone.1), kind=kCustom, calls=%fused_computation.16 | custom fusion | bytes 4194306 | tf_op jit(solution)/shard_map/scatter | solution.py:75
  88.4 1.5 fusion.39
  90.1 1.0 copy.29
  91.1 1.4 fusion.13
  93.1 1.4 fusion.22
  94.5 1.6 copy.33
  96.0 1.2 fusion.38
  97.3 1.3 multiply_reduce_fusion
  98.6 1.3 add_convert_fusion
  99.9 1.4 scatter_custom_fusion.3
  101.3 1.5 scatter_fusion
  103.0 22.6 %all_to_all.34 = bf16[32,2,2048]{2,1,0:T(2,128)(2,1)S(1)} all-to-all(bf16[32,2,2048]{2,1,0:T(2,128)(2,1)S(1)} %reshape.242), channel_id=1, replica_groups=mesh['dp'=16,'expert'=32] {'expert'}, dimensions={0} | all-to-all | bytes 524288 | tf_op jit(solution)/shard_map/all_to_all | solution.py:138
  125.7 2.9 collective-permute-start.1
  128.7 2.5 broadcast_in_dim.68
  131.2 0.7 constant_dynamic-update-slice_fusion.15
  131.9 0.8 collective-permute-done
  132.7 3.0 collective-permute-start.3
  135.7 0.7 constant_dynamic-update-slice_fusion.14
  136.4 0.7 constant_dynamic-update-slice_fusion.13
  137.2 2.6 collective-permute-done.2
  139.8 3.0 collective-permute-start.5
  142.7 0.7 constant_dynamic-update-slice_fusion.12
  143.4 0.7 constant_dynamic-update-slice_fusion.11
  144.2 2.6 collective-permute-done.4
  146.8 3.0 collective-permute-start.7
  149.7 0.7 constant_dynamic-update-slice_fusion.10
  150.4 0.7 constant_dynamic-update-slice_fusion.9
  151.2 2.6 collective-permute-done.6
  153.8 3.0 collective-permute-start.9
  156.7 0.7 constant_dynamic-update-slice_fusion.8
  157.4 0.7 constant_dynamic-update-slice_fusion.7
  158.2 2.6 collective-permute-done.8
  160.8 3.0 collective-permute-start.11
  163.7 0.7 constant_dynamic-update-slice_fusion.6
  164.5 0.7 constant_dynamic-update-slice_fusion.5
  165.2 2.6 collective-permute-done.10
  167.8 3.0 collective-permute-start.13
  170.7 0.7 constant_dynamic-update-slice_fusion.4
  171.5 0.7 constant_dynamic-update-slice_fusion.3
  172.2 2.6 collective-permute-done.12
  174.8 0.7 constant_dynamic-update-slice_fusion.2
  175.5 0.7 constant_dynamic-update-slice_fusion.1
  176.2 5.6 %collective-permute-done.14 = bf16[64,2048]{1,0:T(8,128)(2,1)S(1)} collective-permute-done((bf16[64,2048]{1,0:T(8,128)(2,1)S(1)}, bf16[64,2048]{1,0:T(8,128)(2,1)S(1)}, u32[]{:S(2)}, u32[]{:S(2)}) %collective-permute-start.14) | collective-permute-done | bytes 262176 | tf_op jit(solution)/shard_map/ppermute | solution.py:28
  181.8 0.7 constant_dynamic-update-slice_fusion
  182.5 8.8 %convolution_convert_fusion = bf16[1024,2048]{1,0:T(8,128)(2,1)} fusion(bf16[1024,2048]{1,0:T(8,128)(2,1)} %constant_dynamic-update-slice_fusion, bf16[1,256,2048]{2,1,0:T(8,128)(2,1)S(1)} %copy-done, bf16[1,2048,256]{2,1,0:T(8,128)(2,1)} %param.24, f32[256]{0:T(256)S(1)} %bitcast.66), kind=kOutput, calls=%fused_computation.7 | convolution fusion | flops 2150367232 | bytes 10486784 | tf_op jit(solution)/shard_map/dot_general | solution.py:148
  191.3 0.7 copy-done.5
  192.0 0.9 constant_dynamic-slice_fusion
  192.8 119.7 %all-reduce.2.cloned.1.call-done = bf16[1024,2048]{1,0:T(8,128)(2,1)} async-done(((bf16[1024,2048]{1,0:T(8,128)(2,1)}), bf16[1024,2048]{1,0:T(8,128)(2,1)}) %all-reduce.2.cloned.1.call-update) | async-done | bytes 4194320 | tf_op jit(solution)/shard_map/psum | solution.py:151
  312.5 1.0 add_convert_fusion.1
  313.5 0.9 reshape.244
  314.4 9.8 %all-to-all-start.3 = ((bf16[32,2,2048]{2,1,0:T(2,128)(2,1)}), bf16[32,2,2048]{2,1,0:T(2,128)(2,1)S(1)}, u32[]{:S(2)}, u32[]{:S(2)}) async-start(bf16[32,2,2048]{2,1,0:T(2,128)(2,1)} %reshape.244), calls=%async_computation.3 | async-start | bytes 524288 | tf_op jit(solution)/shard_map/all_to_all | solution.py:155
  324.3 11.5 %all-to-all-done.3 = bf16[32,2,2048]{2,1,0:T(2,128)(2,1)S(1)} async-done(((bf16[32,2,2048]{2,1,0:T(2,128)(2,1)}), bf16[32,2,2048]{2,1,0:T(2,128)(2,1)S(1)}, u32[]{:S(2)}, u32[]{:S(2)}) %all-to-all-start.3) | async-done | bytes 262176 | tf_op jit(solution)/shard_map/all_to_all | solution.py:155
  335.9 1.4 gather_fusion
  337.5 2.2 fusion.16
  (61 shorter events, 3.0 us)
Async XLA Ops:
  6.5 176.0 %copy-start = (bf16[1,256,2048]{2,1,0:T(8,128)(2,1)S(1)}, bf16[1,256,2048]{2,1,0:T(8,128)(2,1)}, u32[]{:S(2)}) copy-start(bf16[1,256,2048]{2,1,0:T(8,128)(2,1)} %param.26) | copy-start | bytes 3145732
  9.4 18.0 %all-to-all-start = ((s32[16,8,1]{1,2,0:T(1,128)}), s32[16,8,1]{1,2,0:T(1,128)S(1)}, u32[]{:S(2)}, u32[]{:S(2)}) async-start(s32[16,8,1]{1,2,0:T(1,128)} %bitcast), calls=%async_computation | async-start | bytes 16384 | tf_op jit(solution)/shard_map/all_to_all | solution.py:73
  19.8 13.3 %copy-start.4 = (s32[128,2]{0,1:T(2,128)S(1)}, s32[128,2]{0,1:T(2,128)}, u32[]{:S(2)}) copy-start(s32[128,2]{0,1:T(2,128)} %param.20) | copy-start | bytes 3076
  19.9 14.3 %copy-start.3 = (s32[1,128]{1,0:T(1,128)S(1)}, s32[1,128]{1,0:T(1,128)}, u32[]{:S(2)}) copy-start(s32[1,128]{1,0:T(1,128)} %param.19) | copy-start | bytes 1540
  27.4 55.0 %all-to-all-start.1 = ((bf16[16,8,8192]{2,1,0:T(8,128)(2,1)}), bf16[16,8,8192]{2,1,0:T(8,128)(2,1)}, u32[]{:S(2)}, u32[]{:S(2)}) async-start(bf16[16,8,8192]{2,1,0:T(8,128)(2,1)} %bitcast.57), calls=%async_computation.1 | async-start | bytes 4194304 | tf_op jit(solution)/shard_map/all_to_all | solution.py:72
  33.1 279.4 %all-reduce.2.cloned.1.call-start = ((), (), s32[]{:S(2)}) async-start(), calls=%async_computation.4 | async-start | bytes 8388608 | tf_op jit(solution)/shard_map/psum | solution.py:151
  93.0 5.6 %copy-start.1 = (f32[2048]{0:T(1024)S(1)}, f32[2048]{0:T(1024)}, u32[]{:S(2)}) copy-start(f32[2048]{0:T(1024)} %param.23) | copy-start | bytes 24580
  93.0 5.6 %copy-start.2 = (f32[2048]{0:T(1024)S(1)}, f32[2048]{0:T(1024)}, u32[]{:S(2)}) copy-start(f32[2048]{0:T(1024)} %param.22) | copy-start | bytes 24580
  125.7 7.0 %collective-permute-start = (bf16[64,2048]{1,0:T(8,128)(2,1)S(1)}, bf16[64,2048]{1,0:T(8,128)(2,1)S(1)}, u32[]{:S(2)}, u32[]{:S(2)}) collective-permute-start(bf16[64,2048]{1,0:T(8,128)(2,1)S(1)} %reshape.243), channel_id=1, source_target_pairs={{0,32},{32,64},{64,96},{96,128},{128,160},{160,192},{192,224},{224... | collective-permute-start | bytes 786440 | tf_op jit(solution)/shard_map/ppermute | solution.py:28
  125.7 7.0 %collective-permute-start.1 = (bf16[64,2048]{1,0:T(8,128)(2,1)S(1)}, bf16[64,2048]{1,0:T(8,128)(2,1)S(1)}, u32[]{:S(2)}, u32[]{:S(2)}) collective-permute-start(bf16[64,2048]{1,0:T(8,128)(2,1)S(1)} %reshape.243), channel_id=1, source_target_pairs={{0,480},{32,0},{64,32},{96,64},{128,96},{160,128},{192,160},{224,1... | collective-permute-start | bytes 786440 | tf_op jit(solution)/shard_map/ppermute | solution.py:33
  131.2 51.3 %copy-start.6 = (f32[1,256]{1,0:T(1,128)S(1)}, f32[1,256]{1,0:T(1,128)}, u32[]{:S(2)}) copy-start(f32[1,256]{1,0:T(1,128)} %param.25) | copy-start | bytes 3076
  132.7 7.0 %collective-permute-start.2 = (bf16[64,2048]{1,0:T(8,128)(2,1)S(1)}, bf16[64,2048]{1,0:T(8,128)(2,1)S(1)}, u32[]{:S(2)}, u32[]{:S(2)}) collective-permute-start(bf16[64,2048]{1,0:T(8,128)(2,1)S(1)} %collective-permute-done), channel_id=1, source_target_pairs={{0,32},{32,64},{64,96},{96,128},{128,160},{160,192},{192,224},{224... | collective-permute-start | bytes 786440 | tf_op jit(solution)/shard_map/ppermute | solution.py:28
  132.7 7.0 %collective-permute-start.3 = (bf16[64,2048]{1,0:T(8,128)(2,1)S(1)}, bf16[64,2048]{1,0:T(8,128)(2,1)S(1)}, u32[]{:S(2)}, u32[]{:S(2)}) collective-permute-start(bf16[64,2048]{1,0:T(8,128)(2,1)S(1)} %collective-permute-done.1), channel_id=1, source_target_pairs={{0,480},{32,0},{64,32},{96,64},{128,96},{160,128},{192,160},{224,1... | collective-permute-start | bytes 786440 | tf_op jit(solution)/shard_map/ppermute | solution.py:33
  139.8 7.0 %collective-permute-start.4 = (bf16[64,2048]{1,0:T(8,128)(2,1)S(1)}, bf16[64,2048]{1,0:T(8,128)(2,1)S(1)}, u32[]{:S(2)}, u32[]{:S(2)}) collective-permute-start(bf16[64,2048]{1,0:T(8,128)(2,1)S(1)} %collective-permute-done.2), channel_id=1, source_target_pairs={{0,32},{32,64},{64,96},{96,128},{128,160},{160,192},{192,224},{224... | collective-permute-start | bytes 786440 | tf_op jit(solution)/shard_map/ppermute | solution.py:28
  139.8 7.0 %collective-permute-start.5 = (bf16[64,2048]{1,0:T(8,128)(2,1)S(1)}, bf16[64,2048]{1,0:T(8,128)(2,1)S(1)}, u32[]{:S(2)}, u32[]{:S(2)}) collective-permute-start(bf16[64,2048]{1,0:T(8,128)(2,1)S(1)} %collective-permute-done.3), channel_id=1, source_target_pairs={{0,480},{32,0},{64,32},{96,64},{128,96},{160,128},{192,160},{224,1... | collective-permute-start | bytes 786440 | tf_op jit(solution)/shard_map/ppermute | solution.py:33
  146.8 7.0 %collective-permute-start.6 = (bf16[64,2048]{1,0:T(8,128)(2,1)S(1)}, bf16[64,2048]{1,0:T(8,128)(2,1)S(1)}, u32[]{:S(2)}, u32[]{:S(2)}) collective-permute-start(bf16[64,2048]{1,0:T(8,128)(2,1)S(1)} %collective-permute-done.4), channel_id=1, source_target_pairs={{0,32},{32,64},{64,96},{96,128},{128,160},{160,192},{192,224},{224... | collective-permute-start | bytes 786440 | tf_op jit(solution)/shard_map/ppermute | solution.py:28
  146.8 7.0 %collective-permute-start.7 = (bf16[64,2048]{1,0:T(8,128)(2,1)S(1)}, bf16[64,2048]{1,0:T(8,128)(2,1)S(1)}, u32[]{:S(2)}, u32[]{:S(2)}) collective-permute-start(bf16[64,2048]{1,0:T(8,128)(2,1)S(1)} %collective-permute-done.5), channel_id=1, source_target_pairs={{0,480},{32,0},{64,32},{96,64},{128,96},{160,128},{192,160},{224,1... | collective-permute-start | bytes 786440 | tf_op jit(solution)/shard_map/ppermute | solution.py:33
  153.8 7.0 %collective-permute-start.8 = (bf16[64,2048]{1,0:T(8,128)(2,1)S(1)}, bf16[64,2048]{1,0:T(8,128)(2,1)S(1)}, u32[]{:S(2)}, u32[]{:S(2)}) collective-permute-start(bf16[64,2048]{1,0:T(8,128)(2,1)S(1)} %collective-permute-done.6), channel_id=1, source_target_pairs={{0,32},{32,64},{64,96},{96,128},{128,160},{160,192},{192,224},{224... | collective-permute-start | bytes 786440 | tf_op jit(solution)/shard_map/ppermute | solution.py:28
  153.8 7.0 %collective-permute-start.9 = (bf16[64,2048]{1,0:T(8,128)(2,1)S(1)}, bf16[64,2048]{1,0:T(8,128)(2,1)S(1)}, u32[]{:S(2)}, u32[]{:S(2)}) collective-permute-start(bf16[64,2048]{1,0:T(8,128)(2,1)S(1)} %collective-permute-done.7), channel_id=1, source_target_pairs={{0,480},{32,0},{64,32},{96,64},{128,96},{160,128},{192,160},{224,1... | collective-permute-start | bytes 786440 | tf_op jit(solution)/shard_map/ppermute | solution.py:33
  160.8 7.0 %collective-permute-start.10 = (bf16[64,2048]{1,0:T(8,128)(2,1)S(1)}, bf16[64,2048]{1,0:T(8,128)(2,1)S(1)}, u32[]{:S(2)}, u32[]{:S(2)}) collective-permute-start(bf16[64,2048]{1,0:T(8,128)(2,1)S(1)} %collective-permute-done.8), channel_id=1, source_target_pairs={{0,32},{32,64},{64,96},{96,128},{128,160},{160,192},{192,224},{224... | collective-permute-start | bytes 786440 | tf_op jit(solution)/shard_map/ppermute | solution.py:28
  160.8 7.0 %collective-permute-start.11 = (bf16[64,2048]{1,0:T(8,128)(2,1)S(1)}, bf16[64,2048]{1,0:T(8,128)(2,1)S(1)}, u32[]{:S(2)}, u32[]{:S(2)}) collective-permute-start(bf16[64,2048]{1,0:T(8,128)(2,1)S(1)} %collective-permute-done.9), channel_id=1, source_target_pairs={{0,480},{32,0},{64,32},{96,64},{128,96},{160,128},{192,160},{224,1... | collective-permute-start | bytes 786440 | tf_op jit(solution)/shard_map/ppermute | solution.py:33
  167.8 7.0 %collective-permute-start.12 = (bf16[64,2048]{1,0:T(8,128)(2,1)S(1)}, bf16[64,2048]{1,0:T(8,128)(2,1)S(1)}, u32[]{:S(2)}, u32[]{:S(2)}) collective-permute-start(bf16[64,2048]{1,0:T(8,128)(2,1)S(1)} %collective-permute-done.10), channel_id=1, source_target_pairs={{0,32},{32,64},{64,96},{96,128},{128,160},{160,192},{192,224},{224... | collective-permute-start | bytes 786440 | tf_op jit(solution)/shard_map/ppermute | solution.py:28
  167.8 7.7 %collective-permute-start.13 = (bf16[64,2048]{1,0:T(8,128)(2,1)S(1)}, bf16[64,2048]{1,0:T(8,128)(2,1)S(1)}, u32[]{:S(2)}, u32[]{:S(2)}) collective-permute-start(bf16[64,2048]{1,0:T(8,128)(2,1)S(1)} %collective-permute-done.11), channel_id=1, source_target_pairs={{0,480},{32,0},{64,32},{96,64},{128,96},{160,128},{192,160},{224,1... | collective-permute-start | bytes 786440 | tf_op jit(solution)/shard_map/ppermute | solution.py:33
  174.8 7.0 %collective-permute-start.14 = (bf16[64,2048]{1,0:T(8,128)(2,1)S(1)}, bf16[64,2048]{1,0:T(8,128)(2,1)S(1)}, u32[]{:S(2)}, u32[]{:S(2)}) collective-permute-start(bf16[64,2048]{1,0:T(8,128)(2,1)S(1)} %collective-permute-done.12), channel_id=1, source_target_pairs={{0,32},{32,64},{64,96},{96,128},{128,160},{160,192},{192,224},{224... | collective-permute-start | bytes 786440 | tf_op jit(solution)/shard_map/ppermute | solution.py:28
  191.3 0.7 copy-start.5
  314.4 21.4 %all-to-all-start.3 = ((bf16[32,2,2048]{2,1,0:T(2,128)(2,1)}), bf16[32,2,2048]{2,1,0:T(2,128)(2,1)S(1)}, u32[]{:S(2)}, u32[]{:S(2)}) async-start(bf16[32,2,2048]{2,1,0:T(2,128)(2,1)} %reshape.244), calls=%async_computation.3 | async-start | bytes 524288 | tf_op jit(solution)/shard_map/all_to_all | solution.py:155
Sparse Core Ops, SparseCore 0:
  191.4 121.0 all-reduce.1
